TPU v7x, 128 devices: a whole 4x4x4 slice. The times are simulated.
128 devices in a mesh: blk: 16 (over x_hi, z, core), tile: 8 (over x_lo, y).
Axes of the slice: x: 4 (x_hi: 2, x_lo: 2; x = x_hi * 2 + x_lo), y: 4, z: 4, core: 2. Of those that a mesh axis runs over, the one named last changes fastest.
Arguments:
- features: bfloat16 [8192, 8192], P('tile', 'blk'), may hold values from -6 to 6
- weight_kv: bfloat16 [8192, 12288], P(None, 'blk'), may hold values from -0.0625 to 0.0625
- key_gain: float32 [6, 128], replicated, may hold values from 0.1 to 1.9
- block_reader: int32 [64], P('tile'), may hold values from 0 to 7, as said below
Outputs:
- routed_kv: bfloat16 [32768, 12288], P('tile', 'blk')
Inputs may be any that keep to these rules, and one draw needn't show every extreme that they name: `block_reader`: at most 4 of the 8 blocks of one index of tile name the same reader, and one reader is named by exactly 4 blocks of every index of tile.
All inputs are finite; a program needn't handle non-finite values.
Results may differ from a plain program's by a relative error of at most 0.001.
Values may be sent and summed in bfloat16 or wider, within the bound.
A program may use at most 192 MiB of HBM per device.

v0:
```python
import jax
import jax.numpy as jnp
from jax import lax
from jax.sharding import PartitionSpec as P

KVH = 8
HD = 128
L = 6
BT = 128
CAP = 4


norm_eps = 1e-05


def local_slots(readers, tile_count):
    onehot = (readers[:, None] == jnp.arange(tile_count, dtype=jnp.int32)[None, :]).astype(
        jnp.int32
    )
    earlier = jnp.cumsum(onehot, axis=0) - onehot
    slot_rank = jnp.sum(earlier * onehot, axis=1)
    return readers * CAP + slot_rank


def shards(features, weight_kv, key_gain, block_reader):
    row_count, feat_local = features.shape
    col_count = weight_kv.shape[1]
    pair_count = col_count // (2 * HD)
    tile_count = lax.axis_size("tile")
    block_count = row_count // BT
    layer_ids = (
        lax.axis_index("blk") * pair_count + jnp.arange(pair_count, dtype=jnp.int32)
    ) // KVH
    layer_pick = (layer_ids[:, None] == jnp.arange(L, dtype=jnp.int32)[None, :]).astype(jnp.float32)
    key_gains = jnp.dot(layer_pick, key_gain, precision=lax.Precision.HIGHEST)
    slot_index = local_slots(block_reader, tile_count)
    selector = (
        slot_index[None, :] == jnp.arange(tile_count * CAP, dtype=jnp.int32)[:, None]
    ).astype(jnp.bfloat16)
    slot_rows = tile_count * CAP * BT
    running = jnp.dot(
        lax.all_gather(features, "blk", axis=1, tiled=True),
        weight_kv,
        preferred_element_type=jnp.float32,
    )
    count = running.shape[0]
    halves = running.reshape(count, pair_count, 2, HD)
    key_part = halves[:, :, 0]
    mean_square = jnp.mean(key_part * key_part, axis=-1, keepdims=True)
    key_part = key_part * lax.rsqrt(mean_square + norm_eps) * key_gains[None]
    joined = jnp.stack([key_part, halves[:, :, 1]], axis=2)
    key_value = joined.reshape(count, col_count).astype(jnp.bfloat16)
    outgoing = jnp.dot(
        selector, key_value.reshape(block_count, BT * col_count), preferred_element_type=jnp.float32
    )
    outgoing = outgoing.astype(jnp.bfloat16).reshape(slot_rows, col_count)
    routed = lax.all_to_all(outgoing, "tile", split_axis=0, concat_axis=0, tiled=True)
    return routed


def solution(mesh):
    return jax.shard_map(
        shards,
        mesh=mesh,
        in_specs=(P("tile", "blk"), P(None, "blk"), P(), P("tile")),
        out_specs=P("tile", "blk"),
        check_vma=False,
    )
```

profile of v0, /device:TPU:0, one launch (start us, length us, event | category | flops | bytes accessed | tf_op | source)
XLA Modules:
  0.0 278.6 jit_solution(7639619202823156865)
XLA Ops:
  6.5 0.0 copy-start
  6.5 0.0 all-gather.2.cloned.1.call-start
  6.5 0.7 all-gather.2.cloned.1.call-update
  7.3 0.7 fusion.1
  8.0 0.8 select_reduce_fusion
  8.9 0.7 multiply_add_fusion
  9.5 0.0 copy-done
  9.5 0.2 fusion.2
  9.7 121.5 %all-gather.2.cloned.1.call-done = bf16[1024,8192]{1,0:T(8,128)(2,1)} async-done(((bf16[1024,512]{1,0:T(8,128)(2,1)}), bf16[1024,8192]{1,0:T(8,128)(2,1)}) %all-gather.2.cloned.1.call-update) | async-done | bytes 16777232 | tf_op jit(solution)/shard_map/all_gather | solution.py:42
  131.2 20.3 %fusion.4 = f32[1024,768]{0,1:T(8,128)} fusion(bf16[1024,8192]{1,0:T(8,128)(2,1)} %all-gather.2.cloned.1.call-done, bf16[8192,768]{1,0:T(8,128)(2,1)} %param.5), kind=kOutput, calls=%fused_computation.18 | convolution fusion | flops 12884901888 | bytes 32505856 | tf_op jit(solution)/shard_map/dot_general | solution.py:41
  151.5 1.5 slice.9
  153.0 2.4 slice.10
  155.4 1.7 copy.16
  157.2 5.7 %multiply_reduce_fusion = f32[1024,3]{1,0:T(8,128)S(1)} fusion(f32[1024,3,1,128]{3,2,1,0:T(1,128)S(1)} %copy.16), kind=kLoop, calls=%fused_computation.3 | loop fusion | flops 783360 | bytes 1585152 | tf_op jit(solution)/shard_map/reduce_sum | solution.py:49
  162.9 0.9 add_rsqrt_fusion
  163.8 4.1 %copy.17 = bf16[1024,3,1,128]{3,2,1,0:T(2,128)(2,1)S(1)} copy(bf16[1024,3,1,128]{0,3,2,1:T(8,128)(2,1)} %slice.10) | data formatting | bytes 1572864
  167.9 8.0 %multiply_convert_fusion = bf16[1024,3,1,128]{3,2,1,0:T(2,128)(2,1)S(1)} fusion(f32[1024,3,1,128]{3,2,1,0:T(1,128)S(1)} %copy.16, f32[3,128]{1,0:T(4,128)S(1)} %fusion.2, f32[1024,3]{1,0:T(8,128)} %add_rsqrt_fusion), kind=kLoop, calls=%fused_computation.2 | loop fusion | flops 1179648 | bytes 2373120 | tf_op jit(solution)/shard_map/convert
  176.0 3.6 %pad_maximum_fusion = bf16[1024,3,2,128]{3,2,1,0:T(2,128)(2,1)S(1)} fusion(bf16[1024,3,1,128]{3,2,1,0:T(2,128)(2,1)S(1)} %copy.17, bf16[1024,3,1,128]{3,2,1,0:T(2,128)(2,1)S(1)} %multiply_convert_fusion), kind=kLoop, calls=%fused_computation.1 | loop fusion | flops 3145728 | bytes 3145728 | tf_op jit(solution)/shard_map/stack | solution.py:51
  179.6 1.2 convert_element_type.14
  180.8 4.5 %convolution_convert_fusion = bf16[32,98304]{1,0:T(8,128)(2,1)} fusion(bf16[8,98304]{1,0:T(8,128)(2,1)S(1)} %convert_element_type.14, s32[8]{0:T(128)S(1)} %multiply_add_fusion), kind=kOutput, calls=%fused_computation | convolution fusion | flops 53477632 | bytes 7864352 | tf_op jit(solution)/shard_map/dot_general | solution.py:53
  185.3 7.3 %all_to_all.8 = bf16[8,512,768]{2,1,0:T(8,128)(2,1)} reshape(bf16[32,98304]{1,0:T(8,128)(2,1)} %convolution_convert_fusion) | data formatting | bytes 12582912 | tf_op jit(solution)/shard_map/all_to_all | solution.py:57
  192.5 76.5 %all_to_all.12 = bf16[8,512,768]{2,1,0:T(8,128)(2,1)S(1)} all-to-all(bf16[8,512,768]{2,1,0:T(8,128)(2,1)} %all_to_all.8), channel_id=1, replica_groups=mesh['blk'=16,'tile'=8] {'tile'}, dimensions={0} | all-to-all | bytes 12582912 | tf_op jit(solution)/shard_map/all_to_all | solution.py:57
  269.1 0.0 copy-start.1
  269.1 2.7 copy.20
  271.8 0.0 copy-done.1
  (2 shorter events, 0.0 us)
Async XLA Ops:
  6.5 3.0 %copy-start = (f32[6,128]{1,0:T(8,128)S(1)}, f32[6,128]{1,0:T(8,128)}, u32[]{:S(2)}) copy-start(f32[6,128]{1,0:T(8,128)} %param.6) | copy-start | bytes 9220
  6.5 124.7 %all-gather.2.cloned.1.call-start = ((), (), s32[]{:S(2)}) async-start(), calls=%async_computation.1 | async-start | bytes 17825792 | tf_op jit(solution)/shard_map/all_gather | solution.py:42
  269.1 2.7 copy-start.1
Sparse Core Ops, SparseCore 0:
  9.6 121.5 all-gather.1
where the time goes:
time: 279 us
  waiting for transfers between devices  122 us (44%)
  blocking collectives  76.5 us (27%)
  matrix products  24.9 us (9%)
  local copies, waits for them, and re-layouts  21 us (8%)
  other arithmetic  20.5 us (7%)
  between operations  13.4 us (5%)
    all_gather x1, waiting for transfers between devices, shards(): lax.all_gather(features, 'blk', axis=1, tiled=True)  122 us
    all_to_all x1, blocking collectives, shards(): lax.all_to_all(outgoing, 'tile', split_axis=0, concat_axis=0, tiled=True)  76.5 us
    dot_general x1, matrix products, shards(): jnp.dot(lax.all_gather(features, 'blk', axis=1, tiled=True), weight_kv, p...  20.3 us
    unnamed x7, local copies, waits for them, and re-layouts  8.58 us
    another operation x1, other arithmetic  8.05 us
    all_to_all x1, local copies, waits for them, and re-layouts, shards(): lax.all_to_all(outgoing, 'tile', split_axis=0, concat_axis=0, tiled=True)  7.28 us
    reduce_sum x1, other arithmetic, shards(): mean_square = jnp.mean(key_part * key_part, axis=-1, keepdims=True)  5.71 us
  transfers between devices with their start and end apart: 1, of which 1 were waited for; matrix products, arithmetic and copies ran while one was open for 1% of the time, Pallas kernels for 0%

commit v1 on v0

v1 whole, which is shorter than its diff:
```python
import jax
import jax.numpy as jnp
from jax import lax
from jax.experimental import pallas as pl
from jax.experimental.pallas import tpu as pltpu
from jax.sharding import PartitionSpec as P

KVH = 8
HD = 128
BT = 128
BPS = 8
CAP = 4
Q = 8
HALF = 64
ROWS = 2 * HALF
PIECE = 512
WIDTH = 8192
COLS = 768
PAIRS = 3

norm_eps = 1e-05


def device(h, z, c, l, y):
    return {"blk": (h * 4 + z) * 2 + c, "tile": l * 4 + y}


def kv_kernel(x_ref, w_hbm, gain_ref, br_ref, cand_ref, meta_out, feats, w_ref, kv, near, pay_own, pay_near,
              meta_v, meta_s, link_send, link_recv, sib_recv, near_recv, y_send, y_recv, meta_send, meta_recv,
              local_sem, w_sem, smem_sem):
    b = lax.axis_index("blk")
    t = lax.axis_index("tile")
    h, z, c = b // 8, (b // 2) % 4, b % 2
    l, y = t // 4, t % 4
    zp, zm, z2 = (z + 1) % 4, (z + 3) % 4, (z + 2) % 4
    h2 = 1 - h
    other = (1 - l) * 4 + y

    w_copy = pltpu.make_async_copy(w_hbm, w_ref, w_sem)
    w_copy.start()

    barrier = pltpu.get_barrier_semaphore()
    friends = [device(h2, z, c, l, y), device(h, zp, c, l, y), device(h, zm, c, l, y), device(h, z, 1 - c, l, y)]
    peers = []
    for dl in range(2):
        for dy in range(4):
            if dl or dy:
                peers.append(device(h, z, c, (l + dl) % 2, (y + dy) % 4))
    for d in friends + peers:
        pl.semaphore_signal(barrier, inc=1, device_id=d, device_id_type=pl.DeviceIdType.MESH)

    br = [br_ref[k] for k in range(BPS)]
    heavy = jnp.int32(0)
    for r in reversed(range(8)):
        count = sum((br[k] == r).astype(jnp.int32) for k in range(BPS))
        heavy = jnp.where(count == CAP, jnp.int32(r), heavy)
    h_block = [jnp.int32(0)] * CAP
    r_block = [jnp.int32(0)] * CAP
    r_reader = [jnp.int32(0)] * CAP
    h_seen, r_seen = jnp.int32(0), jnp.int32(0)
    for k in range(BPS):
        is_h = (br[k] == heavy).astype(jnp.int32)
        for j in range(CAP):
            take_h = is_h * (h_seen == j).astype(jnp.int32)
            take_r = (1 - is_h) * (r_seen == j).astype(jnp.int32)
            h_block[j] = h_block[j] + take_h * k
            r_block[j] = r_block[j] + take_r * k
            r_reader[j] = r_reader[j] + take_r * br[k]
        h_seen = h_seen + is_h
        r_seen = r_seen + (1 - is_h)

    def cols(piece):
        return pl.ds(pl.multiple_of(piece * PIECE, PIECE), PIECE)

    for i in range(CAP):
        for half in range(2):
            q = 2 * i + half
            feats[q, 0:HALF, cols(b)] = x_ref[2 * h_block[i] + half]
            feats[q, HALF:ROWS, cols(b)] = x_ref[2 * r_block[i] + half]
    row = lax.broadcasted_iota(jnp.int32, (8, 128), 0)
    info = jnp.where(row == 4, heavy, 0)
    for j in range(CAP):
        info = jnp.where(row == j, r_reader[j], info)
    meta_v[t] = info

    pl.semaphore_wait(barrier, len(friends) + len(peers))

    def piece_of(ph, pz, pc):
        return (ph * 4 + pz) * 2 + pc

    def view(q, piece):
        return feats.at[q, :, cols(piece)]

    def remote(src, dst, ss, rs, d):
        return pltpu.make_async_remote_copy(src_ref=src, dst_ref=dst, send_sem=ss, recv_sem=rs, device_id=d,
                                            device_id_type=pl.DeviceIdType.MESH)

    to_h = device(h2, z, c, l, y)
    to_p = device(h, zp, c, l, y)
    to_m = device(h, zm, c, l, y)
    to_c = device(h, z, 1 - c, l, y)
    own = piece_of(h, z, c)
    got = [piece_of(h2, z, c), piece_of(h, zm, c), piece_of(h, zp, c), piece_of(h2, zm, c), piece_of(h2, zp, c),
           piece_of(h, z2, c), piece_of(h2, z2, c)]

    def link(q, piece, kind, d):
        remote(view(q, piece), view(q, piece), link_send.at[kind], link_recv.at[q, kind], d).start()

    def arrived(q, kind):
        v = view(q, got[kind])
        remote(v, v, link_send.at[kind], link_recv.at[q, kind], to_p).wait_recv()

    def sib(q, piece):
        remote(view(q, piece), view(q, piece), link_send.at[7], sib_recv.at[q], to_c).start()

    def begin(q):
        link(q, own, 0, to_h)
        link(q, own, 1, to_p)
        link(q, own, 2, to_m)
        sib(q, own)

    def y_dev(dy):
        return device(h, z, c, l, (y + dy) % 4)

    def spread(q, pay, which, source):
        for dy in (2, 1, 3):
            remote(pay.at[q, dy], cand_ref.at[source, q], y_send.at[which, dy], y_recv.at[which, dy], y_dev(dy)).start()
        pltpu.make_async_copy(pay.at[q, 0], cand_ref.at[source, q], local_sem.at[which]).start()

    begin(0)
    metas = []
    for i, d in enumerate(peers):
        dl, dy = (i + 1) // 4, (i + 1) % 4
        cp = remote(meta_v.at[t], meta_v.at[t], meta_send.at[i], meta_recv.at[i], d)
        cp.start()
        metas.append((dl, dy))

    def step(k, carry):
        @pl.when(k + 1 < Q)
        def _():
            begin(k + 1)

        @pl.when(k < Q)
        def _():
            arrived(k, 0)
            link(k, got[0], 3, to_p)
            link(k, got[0], 4, to_m)
            sib(k, got[0])
            arrived(k, 1)
            link(k, got[1], 5, to_p)
            sib(k, got[1])
            arrived(k, 4)
            link(k, got[4], 6, to_m)
            sib(k, got[4])

        @pl.when((k >= 1) & (k < Q + 1))
        def _():
            for kind in (2, 3, 5, 6):
                arrived(k - 1, kind)
                sib(k - 1, got[kind])

        @pl.when(k == 2)
        def _():
            w_copy.wait()
            for i, (dl, dy) in enumerate(metas):
                source = ((l + dl) % 2) * 4 + (y - dy + 4) % 4
                remote(meta_v.at[source], meta_v.at[source], meta_send.at[i], meta_recv.at[i], to_p).wait()
            to_s = pltpu.make_async_copy(meta_v, meta_s, smem_sem)
            to_s.start()
            to_s.wait()

        @pl.when((k >= 2) & (k < Q + 2))
        def _():
            q = k - 2
            both = feats.at[q, :, 0:WIDTH // 2]
            remote(both, both, link_send.at[7], sib_recv.at[q], to_c).wait_recv()
            for j in range(PAIRS):
                at = slice(j * 2 * HD, (j + 1) * 2 * HD)
                acc = jnp.dot(feats[q], w_ref[:, at], preferred_element_type=jnp.float32)
                key = acc[:, :HD]
                layer = (b * PAIRS + j) // KVH
                scale = lax.rsqrt(jnp.mean(key * key, axis=-1, keepdims=True) + norm_eps)
                key = key * scale * gain_ref[pl.ds(layer, 1), :]
                both_kv = jnp.concatenate([key, acc[:, HD:]], axis=1).astype(jnp.bfloat16)
                h_part, r_part = both_kv[:HALF], both_kv[HALF:]
                kv[q, 0, :, at] = h_part
                kv[q, 1, :, at] = r_part
                for dy in range(4):
                    mine = heavy == l * 4 + (y + dy) % 4
                    pay_own[q, dy, :, at] = jnp.where(mine, h_part, r_part)

        @pl.when((k >= 3) & (k < Q + 3))
        def _():
            q = k - 3
            remote(near.at[q], near.at[q], link_send.at[8], near_recv.at[q], to_p).wait_recv()
            near_heavy = meta_s[other, 4, 0]
            h_part, r_part = near[q, 0], near[q, 1]
            for dy in range(4):
                mine = near_heavy == l * 4 + (y + dy) % 4
                pay_near[q, dy] = jnp.where(mine, h_part, r_part)

        @pl.when((k >= 2) & (k < Q + 2))
        def _():
            q = k - 2
            remote(kv.at[q], near.at[q], link_send.at[8], near_recv.at[q], device(h, z, c, 1 - l, y)).start()
            spread(q, pay_own, 0, t)

        @pl.when((k >= 3) & (k < Q + 3))
        def _():
            spread(k - 3, pay_near, 1, other)

        return carry

    lax.fori_loop(0, Q + 3, step, 0)
    meta_out[...] = meta_v[...]

    one = feats.at[:, :, 0:PIECE]
    for kind in range(7):
        remote(one, one, link_send.at[kind], link_recv.at[0, kind], to_p).wait_send()
    eight = feats.at[:, :, 0:WIDTH // 2]
    remote(eight, eight, link_send.at[7], sib_recv.at[0], to_c).wait_send()
    remote(kv, near, link_send.at[8], near_recv.at[0], to_p).wait_send()
    for which, pay in ((0, pay_own), (1, pay_near)):
        for dy in (1, 2, 3):
            source = (l if which == 0 else 1 - l) * 4 + (y - dy + 4) % 4
            cp = remote(pay.at[:, dy], cand_ref.at[source], y_send.at[which, dy], y_recv.at[which, dy], to_p)
            cp.wait_send()
            cp.wait_recv()
        pltpu.make_async_copy(pay.at[:, 0], cand_ref.at[t if which == 0 else other], local_sem.at[which]).wait()


def place_kernel(meta_ref, cand_ref, out_ref):
    t = lax.axis_index("tile")
    is_h = (meta_ref[0, 4, 0] == t).astype(jnp.int32)
    pick = [is_h * c for c in range(CAP)]
    used = [is_h] * CAP
    seen = jnp.int32(0)
    for j in range(CAP):
        named = (1 - is_h) * (meta_ref[0, j, 0] == t).astype(jnp.int32)
        for c in range(CAP):
            hit = named * (seen == c).astype(jnp.int32)
            pick[c] = pick[c] + hit * j
            used[c] = used[c] + hit
        seen = seen + named
    for c in range(CAP):
        block = cand_ref[0, pick[c]]
        out_ref[0, c] = jnp.where(used[c] > 0, block, jnp.zeros_like(block))


def shards(features, weight_kv, key_gain, block_reader):
    dma = pltpu.SemaphoreType.DMA
    bf16 = jnp.bfloat16
    vmem = pl.BlockSpec(memory_space=pltpu.VMEM)
    hbm = pl.BlockSpec(memory_space=pl.ANY)
    cand, meta = pl.pallas_call(
        kv_kernel,
        out_shape=(
            jax.ShapeDtypeStruct((8, Q, HALF, COLS), bf16),
            jax.ShapeDtypeStruct((8, 8, 128), jnp.int32),
        ),
        in_specs=[vmem, hbm, vmem, pl.BlockSpec(memory_space=pltpu.SMEM)],
        out_specs=(hbm, vmem),
        scratch_shapes=[
            pltpu.VMEM((Q, ROWS, WIDTH), bf16),
            pltpu.VMEM((WIDTH, COLS), bf16),
            pltpu.VMEM((Q, 2, HALF, COLS), bf16),
            pltpu.VMEM((Q, 2, HALF, COLS), bf16),
            pltpu.VMEM((Q, 4, HALF, COLS), bf16),
            pltpu.VMEM((Q, 4, HALF, COLS), bf16),
            pltpu.VMEM((8, 8, 128), jnp.int32),
            pltpu.SMEM((8, 8, 128), jnp.int32),
            dma((9,)),
            dma((Q, 7)),
            dma((Q,)),
            dma((Q,)),
            dma((2, 4)),
            dma((2, 4)),
            dma((7,)),
            dma((7,)),
            dma((2,)),
            dma,
            dma,
        ],
        compiler_params=pltpu.CompilerParams(
            collective_id=0, has_side_effects=True, vmem_limit_bytes=60 * 2**20
        ),
        name="gather_project_route",
    )(features.reshape(16, HALF, PIECE), weight_kv, key_gain, block_reader)
    slots = pl.pallas_call(
        place_kernel,
        grid=(8,),
        out_shape=jax.ShapeDtypeStruct((8, CAP, BT, COLS), bf16),
        in_specs=[
            pl.BlockSpec((1, 8, 128), lambda s: (s, 0, 0), memory_space=pltpu.SMEM),
            pl.BlockSpec((1, CAP, BT, COLS), lambda s: (s, 0, 0, 0)),
        ],
        out_specs=pl.BlockSpec((1, CAP, BT, COLS), lambda s: (s, 0, 0, 0)),
        name="place_slots",
    )(meta, cand.reshape(8, CAP, BT, COLS))
    return slots.reshape(8 * CAP * BT, COLS)


def solution(mesh):
    return jax.shard_map(
        shards,
        mesh=mesh,
        in_specs=(P("tile", "blk"), P(None, "blk"), P(), P("tile")),
        out_specs=P("tile", "blk"),
        check_vma=False,
    )
```

time: 279 us -> 127 us (0.46)
  Pallas kernels: 0 us -> 127 us
  waiting for transfers between devices: 122 us -> 0 us
  blocking collectives: 76.5 us -> 0 us
  matrix products: 24.9 us -> 0 us
  local copies, waits for them, and re-layouts: 21 us -> 0 us
  other arithmetic: 20.5 us -> 0 us
  between operations: 13.4 us -> 0.01 us
    pallas_call x0 -> x2, Pallas kernels: none -> 127 us  [the longest x1 119 us: shards(): pl.pallas_call(kv_kernel, out_shape=(jax.ShapeDtypeStruct((8, Q, HALF, CO...]
    all_gather x1 -> x0, waiting for transfers between devices: 122 us -> none  [shards(): lax.all_gather(features, 'blk', axis=1, tiled=True)]
    all_to_all x1 -> x0, blocking collectives: 76.5 us -> none  [shards(): lax.all_to_all(outgoing, 'tile', split_axis=0, concat_axis=0, tiled=True)]
    dot_general x3 -> x0, matrix products: 24.9 us -> none  [the longest x1 20.3 us: shards(): jnp.dot(lax.all_gather(features, 'blk', axis=1, tiled=True), weight_kv, p...]
    another operation x3 -> x0, other arithmetic: 11.7 us -> none
    unnamed x7 -> x0, local copies, waits for them, and re-layouts: 8.58 us -> none
    all_to_all x1 -> x0, local copies, waits for them, and re-layouts: 7.28 us -> none  [shards(): lax.all_to_all(outgoing, 'tile', split_axis=0, concat_axis=0, tiled=True)]
    reduce_sum x2 -> x0, other arithmetic: 6.54 us -> none  [the longest x1 5.71 us: shards(): mean_square = jnp.mean(key_part * key_part, axis=-1, keepdims=True)]
  transfers between devices with their start and end apart: 1 -> 0, of which waited for: 1 -> 0; matrix products, arithmetic and copies ran while one was open for 1% -> 0% of each run, Pallas kernels for 0% -> 0%
where the time goes in v1:
time: 127 us
  Pallas kernels  127 us (100%)
    pallas_call x1, Pallas kernels, shards(): pl.pallas_call(kv_kernel, out_shape=(jax.ShapeDtypeStruct((8, Q, HALF, CO...  119 us
    pallas_call x1, Pallas kernels, shards(): pl.pallas_call(place_kernel, grid=(8,), out_shape=jax.ShapeDtypeStruct((8...  8.13 us

profile of v1, /device:TPU:0, one launch (start us, length us, event | category | flops | bytes accessed | tf_op | source)
XLA Modules:
  0.0 126.8 jit_solution(16052103863025051149)
XLA Ops:
  0.0 118.7 %gather_project_route.1 = (bf16[8,8,64,768]{3,2,1,0:T(8,128)(2,1)}, s32[8,8,128]{2,1,0:T(8,128)}) custom-call(bf16[16,64,512]{2,1,0:T(8,128)(2,1)} %bitcast.4, bf16[8192,768]{1,0:T(8,128)(2,1)} %w_hbm.1, f32[6,128]{1,0:T(8,128)} %gain_ref.1, s32[8]{0:T(128)} %br_ref.1), custom_call_target="tpu_custom_call" | custom-call | tf_op jit(solution)/shard_map/gather_project_route/pallas_call | solution.py:255
  118.7 8.1 %place_slots.1 = bf16[8,4,128,768]{3,2,1,0:T(8,128)(2,1)} custom-call(s32[8,8,128]{2,1,0:T(8,128)} %get-tuple-element.7.meta_ref, bf16[8,4,128,768]{3,2,1,0:T(8,128)(2,1)} %bitcast.3), custom_call_target="tpu_custom_call" | custom-call | tf_op jit(solution)/shard_map/place_slots/pallas_call | solution.py:289

commit v2 on v1

--- a/solution.py
+++ b/solution.py
@@ -10,10 +10,12 @@
 BT = 128
 BPS = 8
 CAP = 4
-Q = 8
-HALF = 64
+PARTS = 2
+Q = CAP * PARTS
+HALF = BT // PARTS
 ROWS = 2 * HALF
 PIECE = 512
+PIECES = 16
 WIDTH = 8192
 COLS = 768
 PAIRS = 3
@@ -69,14 +71,11 @@
         h_seen = h_seen + is_h
         r_seen = r_seen + (1 - is_h)
 
-    def cols(piece):
-        return pl.ds(pl.multiple_of(piece * PIECE, PIECE), PIECE)
-
     for i in range(CAP):
-        for half in range(2):
-            q = 2 * i + half
-            feats[q, 0:HALF, cols(b)] = x_ref[2 * h_block[i] + half]
-            feats[q, HALF:ROWS, cols(b)] = x_ref[2 * r_block[i] + half]
+        for part in range(PARTS):
+            q = PARTS * i + part
+            feats[q, b, 0:HALF] = x_ref[PARTS * h_block[i] + part]
+            feats[q, b, HALF:ROWS] = x_ref[PARTS * r_block[i] + part]
     row = lax.broadcasted_iota(jnp.int32, (8, 128), 0)
     info = jnp.where(row == 4, heavy, 0)
     for j in range(CAP):
@@ -89,7 +88,7 @@
         return (ph * 4 + pz) * 2 + pc
 
     def view(q, piece):
-        return feats.at[q, :, cols(piece)]
+        return feats.at[q, piece]
 
     def remote(src, dst, ss, rs, d):
         return pltpu.make_async_remote_copy(src_ref=src, dst_ref=dst, send_sem=ss, recv_sem=rs, device_id=d,
@@ -146,18 +145,29 @@
             link(k, got[0], 3, to_p)
             link(k, got[0], 4, to_m)
             sib(k, got[0])
+
+        @pl.when((k >= 1) & (k < Q + 1))
+        def _():
+            arrived(k - 1, 4)
+            link(k - 1, got[4], 6, to_m)
+            sib(k - 1, got[4])
+
+        @pl.when(k < Q)
+        def _():
             arrived(k, 1)
             link(k, got[1], 5, to_p)
             sib(k, got[1])
-            arrived(k, 4)
-            link(k, got[4], 6, to_m)
-            sib(k, got[4])
 
         @pl.when((k >= 1) & (k < Q + 1))
         def _():
-            for kind in (2, 3, 5, 6):
+            for kind in (2, 3, 5):
                 arrived(k - 1, kind)
                 sib(k - 1, got[kind])
+
+        @pl.when((k >= 2) & (k < Q + 2))
+        def _():
+            arrived(k - 2, 6)
+            sib(k - 2, got[6])
 
         @pl.when(k == 2)
         def _():
@@ -172,11 +182,12 @@
         @pl.when((k >= 2) & (k < Q + 2))
         def _():
             q = k - 2
-            both = feats.at[q, :, 0:WIDTH // 2]
+            both = feats.at[q, 0:PIECES // 2]
             remote(both, both, link_send.at[7], sib_recv.at[q], to_c).wait_recv()
             for j in range(PAIRS):
                 at = slice(j * 2 * HD, (j + 1) * 2 * HD)
-                acc = jnp.dot(feats[q], w_ref[:, at], preferred_element_type=jnp.float32)
+                rows = jnp.concatenate([feats[q, p] for p in range(PIECES)], axis=1)
+                acc = jnp.dot(rows, w_ref[:, at], preferred_element_type=jnp.float32)
                 key = acc[:, :HD]
                 layer = (b * PAIRS + j) // KVH
                 scale = lax.rsqrt(jnp.mean(key * key, axis=-1, keepdims=True) + norm_eps)
@@ -214,10 +225,10 @@
     lax.fori_loop(0, Q + 3, step, 0)
     meta_out[...] = meta_v[...]
 
-    one = feats.at[:, :, 0:PIECE]
+    one = feats.at[:, 0]
     for kind in range(7):
         remote(one, one, link_send.at[kind], link_recv.at[0, kind], to_p).wait_send()
-    eight = feats.at[:, :, 0:WIDTH // 2]
+    eight = feats.at[:, 0:PIECES // 2]
     remote(eight, eight, link_send.at[7], sib_recv.at[0], to_c).wait_send()
     remote(kv, near, link_send.at[8], near_recv.at[0], to_p).wait_send()
     for which, pay in ((0, pay_own), (1, pay_near)):
@@ -229,22 +240,33 @@
         pltpu.make_async_copy(pay.at[:, 0], cand_ref.at[t if which == 0 else other], local_sem.at[which]).wait()
 
 
-def place_kernel(meta_ref, cand_ref, out_ref):
+def place_kernel(meta_ref, cand_ref, out_ref, took, made, read_sem, write_sem):
     t = lax.axis_index("tile")
-    is_h = (meta_ref[0, 4, 0] == t).astype(jnp.int32)
-    pick = [is_h * c for c in range(CAP)]
-    used = [is_h] * CAP
-    seen = jnp.int32(0)
-    for j in range(CAP):
-        named = (1 - is_h) * (meta_ref[0, j, 0] == t).astype(jnp.int32)
+    for s in range(8):
+        pltpu.make_async_copy(cand_ref.at[s], took.at[s], read_sem.at[s]).start()
+
+    def place(s, carry):
+        is_h = (meta_ref[s, 4, 0] == t).astype(jnp.int32)
+        pick = [is_h * c for c in range(CAP)]
+        used = [is_h] * CAP
+        seen = jnp.int32(0)
+        for j in range(CAP):
+            named = (1 - is_h) * (meta_ref[s, j, 0] == t).astype(jnp.int32)
+            for c in range(CAP):
+                hit = named * (seen == c).astype(jnp.int32)
+                pick[c] = pick[c] + hit * j
+                used[c] = used[c] + hit
+            seen = seen + named
+        pltpu.make_async_copy(cand_ref.at[s], took.at[s], read_sem.at[s]).wait()
         for c in range(CAP):
-            hit = named * (seen == c).astype(jnp.int32)
-            pick[c] = pick[c] + hit * j
-            used[c] = used[c] + hit
-        seen = seen + named
-    for c in range(CAP):
-        block = cand_ref[0, pick[c]]
-        out_ref[0, c] = jnp.where(used[c] > 0, block, jnp.zeros_like(block))
+            block = took[s, pick[c]]
+            made[s, c] = jnp.where(used[c] > 0, block, jnp.zeros_like(block))
+        pltpu.make_async_copy(made.at[s], out_ref.at[s], write_sem.at[s]).start()
+        return carry
+
+    lax.fori_loop(0, 8, place, 0)
+    for s in range(8):
+        pltpu.make_async_copy(made.at[s], out_ref.at[s], write_sem.at[s]).wait()
 
 
 def shards(features, weight_kv, key_gain, block_reader):
@@ -261,7 +283,7 @@
         in_specs=[vmem, hbm, vmem, pl.BlockSpec(memory_space=pltpu.SMEM)],
         out_specs=(hbm, vmem),
         scratch_shapes=[
-            pltpu.VMEM((Q, ROWS, WIDTH), bf16),
+            pltpu.VMEM((Q, PIECES, ROWS, PIECE), bf16),
             pltpu.VMEM((WIDTH, COLS), bf16),
             pltpu.VMEM((Q, 2, HALF, COLS), bf16),
             pltpu.VMEM((Q, 2, HALF, COLS), bf16),
@@ -285,16 +307,18 @@
             collective_id=0, has_side_effects=True, vmem_limit_bytes=60 * 2**20
         ),
         name="gather_project_route",
-    )(features.reshape(16, HALF, PIECE), weight_kv, key_gain, block_reader)
+    )(features.reshape(BPS * PARTS, HALF, PIECE), weight_kv, key_gain, block_reader)
     slots = pl.pallas_call(
         place_kernel,
-        grid=(8,),
         out_shape=jax.ShapeDtypeStruct((8, CAP, BT, COLS), bf16),
-        in_specs=[
-            pl.BlockSpec((1, 8, 128), lambda s: (s, 0, 0), memory_space=pltpu.SMEM),
-            pl.BlockSpec((1, CAP, BT, COLS), lambda s: (s, 0, 0, 0)),
+        in_specs=[pl.BlockSpec(memory_space=pltpu.SMEM), hbm],
+        out_specs=hbm,
+        scratch_shapes=[
+            pltpu.VMEM((8, CAP, BT, COLS), bf16),
+            pltpu.VMEM((8, CAP, BT, COLS), bf16),
+            dma((8,)),
+            dma((8,)),
         ],
-        out_specs=pl.BlockSpec((1, CAP, BT, COLS), lambda s: (s, 0, 0, 0)),
         name="place_slots",
     )(meta, cand.reshape(8, CAP, BT, COLS))
     return slots.reshape(8 * CAP * BT, COLS)

time: 127 us -> 118 us (0.929); the launches traced: 127 us -> 116 us
  Pallas kernels: 127 us -> 116 us
    pallas_call x1, Pallas kernels: 119 us -> 110 us  [shards(): pl.pallas_call(kv_kernel, out_shape=(jax.ShapeDtypeStruct((8, Q, HALF, CO...]
    pallas_call x1, Pallas kernels: 8.13 us -> 6.67 us  [shards(): pl.pallas_call(place_kernel, out_shape=jax.ShapeDtypeStruct((8, CAP, BT,...]
where the time goes in v2:
time: 118 us; the launch traced here: 116 us
  Pallas kernels  116 us (98%)
    pallas_call x1, Pallas kernels, shards(): pl.pallas_call(kv_kernel, out_shape=(jax.ShapeDtypeStruct((8, Q, HALF, CO...  110 us
    pallas_call x1, Pallas kernels, shards(): pl.pallas_call(place_kernel, out_shape=jax.ShapeDtypeStruct((8, CAP, BT,...  6.67 us

profile of v2, /device:TPU:0, one launch (start us, length us, event | category | flops | bytes accessed | tf_op | source)
XLA Modules:
  0.0 116.4 jit_solution(6764981084127180314)
XLA Ops:
  0.0 109.7 %gather_project_route.1 = (bf16[8,8,64,768]{3,2,1,0:T(8,128)(2,1)}, s32[8,8,128]{2,1,0:T(8,128)}) custom-call(bf16[16,64,512]{2,1,0:T(8,128)(2,1)} %bitcast.4, bf16[8192,768]{1,0:T(8,128)(2,1)} %w_hbm.1, f32[6,128]{1,0:T(8,128)} %gain_ref.1, s32[8]{0:T(128)} %br_ref.1), custom_call_target="tpu_custom_call" | custom-call | tf_op jit(solution)/shard_map/gather_project_route/pallas_call | solution.py:277
  109.7 6.7 %place_slots.1 = bf16[8,4,128,768]{3,2,1,0:T(8,128)(2,1)} custom-call(s32[8,8,128]{2,1,0:T(8,128)} %get-tuple-element.7.meta_ref, bf16[8,4,128,768]{3,2,1,0:T(8,128)(2,1)} %bitcast.3), custom_call_target="tpu_custom_call" | custom-call | tf_op jit(solution)/shard_map/place_slots/pallas_call | solution.py:311

commit v3 on v2

--- a/solution.py
+++ b/solution.py
@@ -10,7 +10,7 @@
 BT = 128
 BPS = 8
 CAP = 4
-PARTS = 2
+PARTS = 4
 Q = CAP * PARTS
 HALF = BT // PARTS
 ROWS = 2 * HALF
@@ -126,7 +126,8 @@
             remote(pay.at[q, dy], cand_ref.at[source, q], y_send.at[which, dy], y_recv.at[which, dy], y_dev(dy)).start()
         pltpu.make_async_copy(pay.at[q, 0], cand_ref.at[source, q], local_sem.at[which]).start()
 
-    begin(0)
+    for k in range(3):
+        begin(k)
     metas = []
     for i, d in enumerate(peers):
         dl, dy = (i + 1) // 4, (i + 1) % 4
@@ -135,9 +136,9 @@
         metas.append((dl, dy))
 
     def step(k, carry):
-        @pl.when(k + 1 < Q)
-        def _():
-            begin(k + 1)
+        @pl.when(k + 3 < Q)
+        def _():
+            begin(k + 3)
 
         @pl.when(k < Q)
         def _():
@@ -179,9 +180,9 @@
             to_s.start()
             to_s.wait()
 
-        @pl.when((k >= 2) & (k < Q + 2))
-        def _():
-            q = k - 2
+        @pl.when((k >= 3) & (k < Q + 3))
+        def _():
+            q = k - 3
             both = feats.at[q, 0:PIECES // 2]
             remote(both, both, link_send.at[7], sib_recv.at[q], to_c).wait_recv()
             for j in range(PAIRS):
@@ -200,9 +201,9 @@
                     mine = heavy == l * 4 + (y + dy) % 4
                     pay_own[q, dy, :, at] = jnp.where(mine, h_part, r_part)
 
-        @pl.when((k >= 3) & (k < Q + 3))
-        def _():
-            q = k - 3
+        @pl.when((k >= 4) & (k < Q + 4))
+        def _():
+            q = k - 4
             remote(near.at[q], near.at[q], link_send.at[8], near_recv.at[q], to_p).wait_recv()
             near_heavy = meta_s[other, 4, 0]
             h_part, r_part = near[q, 0], near[q, 1]
@@ -210,19 +211,19 @@
                 mine = near_heavy == l * 4 + (y + dy) % 4
                 pay_near[q, dy] = jnp.where(mine, h_part, r_part)
 
-        @pl.when((k >= 2) & (k < Q + 2))
-        def _():
-            q = k - 2
+        @pl.when((k >= 3) & (k < Q + 3))
+        def _():
+            q = k - 3
             remote(kv.at[q], near.at[q], link_send.at[8], near_recv.at[q], device(h, z, c, 1 - l, y)).start()
             spread(q, pay_own, 0, t)
 
-        @pl.when((k >= 3) & (k < Q + 3))
-        def _():
-            spread(k - 3, pay_near, 1, other)
+        @pl.when((k >= 4) & (k < Q + 4))
+        def _():
+            spread(k - 4, pay_near, 1, other)
 
         return carry
 
-    lax.fori_loop(0, Q + 3, step, 0)
+    lax.fori_loop(0, Q + 4, step, 0)
     meta_out[...] = meta_v[...]
 
     one = feats.at[:, 0]

time: 118 us -> 114 us (0.966); the launches traced: 116 us -> 114 us
  Pallas kernels: 116 us -> 114 us
    pallas_call x1, Pallas kernels: 110 us -> 107 us  [shards(): pl.pallas_call(kv_kernel, out_shape=(jax.ShapeDtypeStruct((8, Q, HALF, CO...]
where the time goes in v3:
time: 114 us
  Pallas kernels  114 us (100%)
    pallas_call x1, Pallas kernels, shards(): pl.pallas_call(kv_kernel, out_shape=(jax.ShapeDtypeStruct((8, Q, HALF, CO...  107 us
    pallas_call x1, Pallas kernels, shards(): pl.pallas_call(place_kernel, out_shape=jax.ShapeDtypeStruct((8, CAP, BT,...  6.67 us

profile of v3, /device:TPU:0, one launch (start us, length us, event | category | flops | bytes accessed | tf_op | source)
XLA Modules:
  0.0 113.6 jit_solution(6231402289267084066)
XLA Ops:
  0.0 107.0 %gather_project_route.1 = (bf16[8,16,32,768]{3,2,1,0:T(8,128)(2,1)}, s32[8,8,128]{2,1,0:T(8,128)}) custom-call(bf16[32,32,512]{2,1,0:T(8,128)(2,1)} %bitcast.4, bf16[8192,768]{1,0:T(8,128)(2,1)} %w_hbm.1, f32[6,128]{1,0:T(8,128)} %gain_ref.1, s32[8]{0:T(128)} %br_ref.1), custom_call_target="tpu_custom_call" | custom-call | tf_op jit(solution)/shard_map/gather_project_route/pallas_call | solution.py:278
  107.0 6.7 %place_slots.1 = bf16[8,4,128,768]{3,2,1,0:T(8,128)(2,1)} custom-call(s32[8,8,128]{2,1,0:T(8,128)} %get-tuple-element.7.meta_ref, bf16[8,4,128,768]{3,2,1,0:T(8,128)(2,1)} %bitcast.3), custom_call_target="tpu_custom_call" | custom-call | tf_op jit(solution)/shard_map/place_slots/pallas_call | solution.py:312

commit v4 on v3

--- a/solution.py
+++ b/solution.py
@@ -147,11 +147,11 @@
             link(k, got[0], 4, to_m)
             sib(k, got[0])
 
-        @pl.when((k >= 1) & (k < Q + 1))
-        def _():
-            arrived(k - 1, 4)
-            link(k - 1, got[4], 6, to_m)
-            sib(k - 1, got[4])
+        @pl.when((k >= 2) & (k < Q + 2))
+        def _():
+            arrived(k - 2, 4)
+            link(k - 2, got[4], 6, to_m)
+            sib(k - 2, got[4])
 
         @pl.when(k < Q)
         def _():
@@ -159,16 +159,16 @@
             link(k, got[1], 5, to_p)
             sib(k, got[1])
 
-        @pl.when((k >= 1) & (k < Q + 1))
+        @pl.when((k >= 2) & (k < Q + 2))
         def _():
             for kind in (2, 3, 5):
-                arrived(k - 1, kind)
-                sib(k - 1, got[kind])
-
-        @pl.when((k >= 2) & (k < Q + 2))
-        def _():
-            arrived(k - 2, 6)
-            sib(k - 2, got[6])
+                arrived(k - 2, kind)
+                sib(k - 2, got[kind])
+
+        @pl.when((k >= 3) & (k < Q + 3))
+        def _():
+            arrived(k - 3, 6)
+            sib(k - 3, got[6])
 
         @pl.when(k == 2)
         def _():
@@ -180,9 +180,9 @@
             to_s.start()
             to_s.wait()
 
-        @pl.when((k >= 3) & (k < Q + 3))
-        def _():
-            q = k - 3
+        @pl.when((k >= 4) & (k < Q + 4))
+        def _():
+            q = k - 4
             both = feats.at[q, 0:PIECES // 2]
             remote(both, both, link_send.at[7], sib_recv.at[q], to_c).wait_recv()
             for j in range(PAIRS):
@@ -201,9 +201,9 @@
                     mine = heavy == l * 4 + (y + dy) % 4
                     pay_own[q, dy, :, at] = jnp.where(mine, h_part, r_part)
 
-        @pl.when((k >= 4) & (k < Q + 4))
-        def _():
-            q = k - 4
+        @pl.when((k >= 5) & (k < Q + 5))
+        def _():
+            q = k - 5
             remote(near.at[q], near.at[q], link_send.at[8], near_recv.at[q], to_p).wait_recv()
             near_heavy = meta_s[other, 4, 0]
             h_part, r_part = near[q, 0], near[q, 1]
@@ -211,19 +211,19 @@
                 mine = near_heavy == l * 4 + (y + dy) % 4
                 pay_near[q, dy] = jnp.where(mine, h_part, r_part)
 
-        @pl.when((k >= 3) & (k < Q + 3))
-        def _():
-            q = k - 3
+        @pl.when((k >= 4) & (k < Q + 4))
+        def _():
+            q = k - 4
             remote(kv.at[q], near.at[q], link_send.at[8], near_recv.at[q], device(h, z, c, 1 - l, y)).start()
             spread(q, pay_own, 0, t)
 
-        @pl.when((k >= 4) & (k < Q + 4))
-        def _():
-            spread(k - 4, pay_near, 1, other)
+        @pl.when((k >= 5) & (k < Q + 5))
+        def _():
+            spread(k - 5, pay_near, 1, other)
 
         return carry
 
-    lax.fori_loop(0, Q + 4, step, 0)
+    lax.fori_loop(0, Q + 5, step, 0)
     meta_out[...] = meta_v[...]
 
     one = feats.at[:, 0]

time: 114 us -> 113 us (level)
  Pallas kernels: 114 us -> 112 us
    pallas_call x1, Pallas kernels: 107 us -> 106 us  [shards(): pl.pallas_call(kv_kernel, out_shape=(jax.ShapeDtypeStruct((8, Q, HALF, CO...]
where the time goes in v4:
time: 113 us; the launch traced here: 112 us
  Pallas kernels  112 us (99%)
    pallas_call x1, Pallas kernels, shards(): pl.pallas_call(kv_kernel, out_shape=(jax.ShapeDtypeStruct((8, Q, HALF, CO...  106 us
    pallas_call x1, Pallas kernels, shards(): pl.pallas_call(place_kernel, out_shape=jax.ShapeDtypeStruct((8, CAP, BT,...  6.67 us

profile of v4, /device:TPU:0, one launch (start us, length us, event | category | flops | bytes accessed | tf_op | source)
XLA Modules:
  0.0 112.3 jit_solution(3732514170317700920)
XLA Ops:
  0.0 105.7 %gather_project_route.1 = (bf16[8,16,32,768]{3,2,1,0:T(8,128)(2,1)}, s32[8,8,128]{2,1,0:T(8,128)}) custom-call(bf16[32,32,512]{2,1,0:T(8,128)(2,1)} %bitcast.4, bf16[8192,768]{1,0:T(8,128)(2,1)} %w_hbm.1, f32[6,128]{1,0:T(8,128)} %gain_ref.1, s32[8]{0:T(128)} %br_ref.1), custom_call_target="tpu_custom_call" | custom-call | tf_op jit(solution)/shard_map/gather_project_route/pallas_call | solution.py:278
  105.7 6.7 %place_slots.1 = bf16[8,4,128,768]{3,2,1,0:T(8,128)(2,1)} custom-call(s32[8,8,128]{2,1,0:T(8,128)} %get-tuple-element.7.meta_ref, bf16[8,4,128,768]{3,2,1,0:T(8,128)(2,1)} %bitcast.3), custom_call_target="tpu_custom_call" | custom-call | tf_op jit(solution)/shard_map/place_slots/pallas_call | solution.py:312
